TPU v7x, 32 devices: a whole 2x2x4 slice. The times are simulated.
32 devices in a mesh: chan: 8 (over y, x, core), stn: 4 (over z).
Axes of the slice: x: 2, y: 2, z: 4, core: 2. Of those that a mesh axis runs over, the one named last changes fastest.
Arguments:
- measured_correlation: float32 [8, 8, 4096], P('chan', None, 'stn'), may hold values from -3 to 3
- model_correlation: float32 [8, 8, 16, 4096], P('chan', None, None, 'stn'), may hold values from -1.0606601 to 1.0606601
- source_pointing: int32 [16, 1], replicated, may hold values from 0 to 7
- antenna_pairs: int32 [2, 4096], P(None, 'stn'), may hold values from 0 to 511, as said below
- starting_jones_matrices: float32 [8, 8, 8, 512], P('chan'), may hold values from -1 to 2
- starting_polynomial_terms: float32 [3, 8, 8, 512], replicated, may hold values from -1 to 2
- starting_lagrange_scaled: float32 [8, 8, 8, 512], P('chan'), may hold values from -1.5 to 1.5
- augmented_lagrange_rhos: float32 [8], replicated, may hold values from 0.5 to 4
Outputs:
- solved_gains: float32 [8, 8, 8, 512], P('chan', None, None, 'stn')
- solved_dual: float32 [8, 8, 8, 512], P('chan', None, None, 'stn')
- fit_coeffs: float32 [3, 8, 8, 512], P(None, None, None, 'stn')
Inputs may be any that keep to these rules, and one draw needn't show every extreme that they name: `antenna_pairs`: row 0 holds a baseline's first station and row 1 its second, which differs from the first. The first station of every baseline in the i-th aligned block of 1024 baselines lies among stations i * 128 to (i + 1) * 128 - 1. `source_pointing`: every direction holds at least one component.
All inputs are finite; a program needn't handle non-finite values.
Results may differ from a plain program's by a relative error of at most 0.0001.
Values sent between devices are 32-bit elements; how exact they have to be, the bound alone decides.
No kernel may reach another device: no remote copies, remote signals or barrier semaphores. Data moves between devices by JAX's collectives and lax.ppermute only.
A program may use at most 64 MiB of HBM per device.

v0:
```python
from functools import partial
import jax
import jax.numpy as jnp
from jax import lax
from jax.sharding import PartitionSpec as P

CALIB_PATHS = 8
TERMS = 3
STEPS = 2
INNER = 2
student_nu = 2.0
squared_tolerance = 1e-06
highest = lax.Precision.HIGHEST


def entries(stacked):
    return [(stacked[slot_idx], stacked[4 + slot_idx]) for slot_idx in range(4)]


def assemble(matrix):
    return jnp.stack(
        [matrix[slot_idx][0] for slot_idx in range(4)]
        + [matrix[slot_idx][1] for slot_idx in range(4)],
        axis=0,
    )


def flatten(matrix):
    return [matrix[slot_idx][0] for slot_idx in range(4)] + [
        matrix[slot_idx][1] for slot_idx in range(4)
    ]


def multiply_pair(first_pair, second_pair):
    return (
        first_pair[0] * second_pair[0] - first_pair[1] * second_pair[1],
        first_pair[0] * second_pair[1] + first_pair[1] * second_pair[0],
    )


def add_pair(first_pair, second_pair):
    return (first_pair[0] + second_pair[0], first_pair[1] + second_pair[1])


def conjugate(value_pair):
    return (value_pair[0], -value_pair[1])


def matrix_product(factor_one, factor_two):
    return [
        add_pair(
            multiply_pair(factor_one[0], factor_two[0]), multiply_pair(factor_one[1], factor_two[2])
        ),
        add_pair(
            multiply_pair(factor_one[0], factor_two[1]), multiply_pair(factor_one[1], factor_two[3])
        ),
        add_pair(
            multiply_pair(factor_one[2], factor_two[0]), multiply_pair(factor_one[3], factor_two[2])
        ),
        add_pair(
            multiply_pair(factor_one[2], factor_two[1]), multiply_pair(factor_one[3], factor_two[3])
        ),
    ]


def adjoint(matrix):
    return [conjugate(matrix[0]), conjugate(matrix[2]), conjugate(matrix[1]), conjugate(matrix[3])]


def gram_parts(matrix):
    upper_sum = (
        matrix[0][0] * matrix[0][0]
        + matrix[0][1] * matrix[0][1]
        + matrix[1][0] * matrix[1][0]
        + matrix[1][1] * matrix[1][1]
    )
    lower_sum = (
        matrix[2][0] * matrix[2][0]
        + matrix[2][1] * matrix[2][1]
        + matrix[3][0] * matrix[3][0]
        + matrix[3][1] * matrix[3][1]
    )
    cross_term = add_pair(
        multiply_pair(matrix[0], conjugate(matrix[2])),
        multiply_pair(matrix[1], conjugate(matrix[3])),
    )
    return [upper_sum, lower_sum, cross_term[0], cross_term[1]]


def basis_table(channel_count):
    frequency = (2.0 * jnp.arange(channel_count, dtype=jnp.float32) + 1.0) / channel_count - 1.0
    columns = []
    for degree in range(TERMS):
        column = frequency**degree
        for earlier in columns:
            column = column - jnp.sum(earlier * column) / channel_count * earlier
        column = column / jnp.sqrt(jnp.sum(column * column) / channel_count)
        columns.append(column)
    return jnp.stack(columns, axis=1)


def combine_sources(cohere_f, source_pointing):
    member = (
        source_pointing[:, 0][:, None] == jnp.arange(CALIB_PATHS, dtype=jnp.int32)[None, :]
    ).astype(jnp.float32)
    return jnp.einsum("csb,sk->ckb", cohere_f, member, precision=highest)


def channel_state(vis_f, cohere_dir, spectral_jones_matrices, antenna_pairs):
    coherent = entries(cohere_dir)
    first_gain = entries(spectral_jones_matrices[:, :, antenna_pairs[0]])
    second_gain = entries(spectral_jones_matrices[:, :, antenna_pairs[1]])
    toward_first = matrix_product(coherent, adjoint(second_gain))
    own_terms = matrix_product(first_gain, toward_first)
    observed = entries(vis_f)
    residual = [
        (
            observed[slot_idx][0] - jnp.sum(own_terms[slot_idx][0], axis=0),
            observed[slot_idx][1] - jnp.sum(own_terms[slot_idx][1], axis=0),
        )
        for slot_idx in range(4)
    ]
    energy = residual[0][0] * residual[0][0] + residual[0][1] * residual[0][1]
    for slot_idx in range(1, 4):
        energy = (
            energy
            + residual[slot_idx][0] * residual[slot_idx][0]
            + residual[slot_idx][1] * residual[slot_idx][1]
        )
    return (residual, own_terms, toward_first, first_gain, coherent, energy)


def channel_sums(chan_state, weight, first_table, second_table, block_start):
    residual, own_terms, toward_first, first_gain, coherent, energy = chan_state
    target = [
        add_pair((residual[slot_idx][0][None], residual[slot_idx][1][None]), own_terms[slot_idx])
        for slot_idx in range(4)
    ]
    back_terms = matrix_product(first_gain, coherent)
    first_parts = (
        jnp.stack(
            gram_parts(toward_first) + flatten(matrix_product(target, adjoint(toward_first))),
            axis=0,
        )
        * weight
    )
    second_parts = (
        jnp.stack(
            gram_parts(adjoint(back_terms)) + flatten(matrix_product(adjoint(target), back_terms)),
            axis=0,
        )
        * weight
    )
    first_block = jnp.einsum("pkb,bs->pks", first_parts, first_table, precision=highest)
    every_station = jnp.einsum("pkb,bs->pks", second_parts, second_table, precision=highest)
    block_width = first_table.shape[1]
    own_rows = lax.dynamic_slice_in_dim(every_station, block_start, block_width, 2) + first_block
    return lax.dynamic_update_slice_in_dim(every_station, own_rows, block_start, 2)


def jones_estimator(
    least_squares_equations, pivot_spectral_point, spectral_jones_matrices, augmented_lagrange_rhos
):
    augmented_rho_factor = augmented_lagrange_rhos[:, None]
    diag_one = least_squares_equations[0] + augmented_rho_factor
    diag_two = least_squares_equations[1] + augmented_rho_factor
    determinant = (
        diag_one * diag_two
        - least_squares_equations[2] * least_squares_equations[2]
        - least_squares_equations[3] * least_squares_equations[3]
    )
    zero_part = jnp.zeros_like(determinant)
    inverse = [
        (diag_two / determinant, zero_part),
        (-least_squares_equations[2] / determinant, -least_squares_equations[3] / determinant),
        (-least_squares_equations[2] / determinant, least_squares_equations[3] / determinant),
        (diag_one / determinant, zero_part),
    ]
    right_side = entries(
        least_squares_equations[4:] + augmented_rho_factor[None] * pivot_spectral_point
    )
    solution = assemble(matrix_product(right_side, inverse))
    return 0.5 * (spectral_jones_matrices + solution)


def body(
    measured_correlation,
    model_correlation,
    source_pointing,
    antenna_pairs,
    starting_jones_matrices,
    starting_polynomial_terms,
    starting_lagrange_scaled,
    augmented_lagrange_rhos,
):
    local_ch = measured_correlation.shape[0]
    stations = starting_jones_matrices.shape[3]
    block_size = stations // lax.axis_size("stn")
    block_start = lax.axis_index("stn") * block_size
    total_ch = local_ch * lax.axis_size("chan")
    sample_count = total_ch * measured_correlation.shape[2] * lax.axis_size("stn")
    my_basis = lax.dynamic_slice_in_dim(
        basis_table(total_ch), lax.axis_index("chan") * local_ch, local_ch, 0
    )
    cohere_dir = jax.vmap(combine_sources, (0, None))(model_correlation, source_pointing)
    first_table = (
        (antenna_pairs[0] - block_start)[:, None]
        == jnp.arange(block_size, dtype=jnp.int32)[None, :]
    ).astype(jnp.float32)
    second_table = (
        antenna_pairs[1][:, None] == jnp.arange(stations, dtype=jnp.int32)[None, :]
    ).astype(jnp.float32)
    state_fn = jax.vmap(channel_state, (0, 0, 0, None))
    sums_fn = jax.vmap(
        partial(
            channel_sums,
            first_table=first_table,
            second_table=second_table,
            block_start=block_start,
        ),
        (0, 0),
    )
    estimate_routine = jax.vmap(jones_estimator, (0, 0, 0, None))

    def own_block(array):
        return lax.dynamic_slice_in_dim(array, block_start, block_size, 3)

    consensus = jnp.einsum("ft,tcks->fcks", my_basis, starting_polynomial_terms, precision=highest)
    whole_jones_matrix = starting_jones_matrices
    dual_now = starting_lagrange_scaled
    gain_mine = starting_jones_matrices
    pending = None
    fit_now = starting_polynomial_terms
    for step_idx in range(STEPS):
        pivot_antenna = consensus - dual_now
        for inner_idx in range(INNER):
            chan_state = state_fn(
                measured_correlation, cohere_dir, whole_jones_matrix, antenna_pairs
            )
            mean_square = (
                lax.psum(jnp.sum(chan_state[5]), ("chan", "stn")) / sample_count + squared_tolerance
            )
            weight = (student_nu + 2.0) / (student_nu + chan_state[5] / mean_square)
            least_squares_equations = sums_fn(chan_state, weight)
            whole_accumulated_totals = lax.psum(least_squares_equations, "stn")
            whole_jones_matrix = estimate_routine(
                whole_accumulated_totals, pivot_antenna, whole_jones_matrix, augmented_lagrange_rhos
            )
            gain_mine = whole_jones_matrix
        partial_fit = jnp.einsum("ft,fcks->tcks", my_basis, gain_mine + dual_now, precision=highest)
        fit_now = lax.psum(partial_fit, "chan") / total_ch
        consensus = jnp.einsum("ft,tcks->fcks", my_basis, fit_now, precision=highest)
        dual_now = dual_now + gain_mine - consensus
    return (own_block(gain_mine), own_block(dual_now), own_block(fit_now))


def solution(mesh):
    placed = (
        P("chan", None, "stn"),
        P("chan", None, None, "stn"),
        P(),
        P(None, "stn"),
        P("chan", None, None, None),
        P(),
        P("chan", None, None, None),
        P(),
    )
    return jax.shard_map(
        body,
        mesh=mesh,
        in_specs=placed,
        out_specs=(
            P("chan", None, None, "stn"),
            P("chan", None, None, "stn"),
            P(None, None, None, "stn"),
        ),
        check_vma=False,
    )
```

profile of v0, /device:TPU:0, one launch (start us, length us, event | category | flops | bytes accessed | tf_op | source)
XLA Modules:
  0.0 534.8 jit_solution(3968500334893282561)
XLA Ops:
  12.9 9.1 %gather_fusion.1 = f32[1024,8,8]{2,1,0:T(8,128)} fusion(f32[8,8,512]{1,0,2:T(8,128)S(1)} %bitcast.987, s32[1024]{0:T(1024)S(1)} %get-tuple-element.362), kind=kCustom, calls=%fused_computation.1 | custom fusion | bytes 528384 | tf_op jit(solution)/shard_map/vmap()/gather | solution.py:112
  21.9 2.8 copy.209
  24.7 9.1 %gather_fusion = f32[1024,8,8]{2,1,0:T(8,128)} fusion(f32[8,8,512]{1,0,2:T(8,128)S(1)} %bitcast.988, s32[1024]{0:T(1024)S(1)} %get-tuple-element.363), kind=kCustom, calls=%fused_computation | custom fusion | bytes 528384 | tf_op jit(solution)/shard_map/vmap()/gather | solution.py:111
  33.8 2.8 copy.197
  38.6 42.2 %psum.70 = f32[]{:T(128)} all-reduce(f32[]{:T(128)} %fusion.207), channel_id=1, replica_groups=mesh['chan'=8,'stn'=4] {'chan','stn'}, use_global_device_ids=true, to_apply=%region_9.0 | all-reduce | flops 1 | bytes 8 | tf_op jit(solution)/shard_map/psum | solution.py:241
  96.7 27.4 %all-reduce.8.cloned.1.call-done = f32[1,12,8,512]{3,2,1,0:T(8,128)} async-done(((f32[1,12,8,512]{3,2,1,0:T(8,128)}), f32[1,12,8,512]{3,2,1,0:T(8,128)}) %all-reduce.8.cloned.1.call-update) | async-done | bytes 196624 | tf_op jit(solution)/shard_map/psum | solution.py:245
  129.1 9.1 %gather_fusion.3 = f32[1024,8,8]{2,1,0:T(8,128)} fusion(f32[8,8,512]{1,0,2:T(8,128)S(1)} %copy.236, s32[1024]{0:T(1024)S(1)} %get-tuple-element.362), kind=kCustom, calls=%fused_computation.3 | custom fusion | bytes 528384 | tf_op jit(solution)/shard_map/vmap()/gather | solution.py:112
  138.2 9.1 %gather_fusion.2 = f32[1024,8,8]{2,1,0:T(8,128)} fusion(f32[8,8,512]{1,0,2:T(8,128)S(1)} %copy.236, s32[1024]{0:T(1024)S(1)} %get-tuple-element.363), kind=kCustom, calls=%fused_computation.2 | custom fusion | bytes 528384 | tf_op jit(solution)/shard_map/vmap()/gather | solution.py:111
  147.3 2.8 copy.243
  150.2 2.8 copy.237
  153.9 40.5 %psum.72 = f32[]{:T(128)} all-reduce(f32[]{:T(128)} %fusion.206), channel_id=1, replica_groups=mesh['chan'=8,'stn'=4] {'chan','stn'}, use_global_device_ids=true, to_apply=%region_26.0 | all-reduce | flops 1 | bytes 8 | tf_op jit(solution)/shard_map/psum | solution.py:241
  200.9 34.9 %all-reduce.10.cloned.1.call-done = f32[1,12,8,512]{3,2,0,1:T(8,128)} async-done(((f32[1,12,8,512]{3,2,0,1:T(8,128)}), f32[1,12,8,512]{3,2,0,1:T(8,128)}) %all-reduce.10.cloned.1.call-update) | async-done | bytes 196624 | tf_op jit(solution)/shard_map/psum | solution.py:245
  239.4 9.1 %gather_fusion.5 = f32[1024,8,8]{2,1,0:T(8,128)} fusion(f32[8,8,512]{1,0,2:T(8,128)S(1)} %copy.249, s32[1024]{0:T(1024)S(1)} %get-tuple-element.362), kind=kCustom, calls=%fused_computation.5 | custom fusion | bytes 528384 | tf_op jit(solution)/shard_map/vmap()/gather | solution.py:112
  248.5 9.1 %gather_fusion.4 = f32[1024,8,8]{2,1,0:T(8,128)} fusion(f32[8,8,512]{1,0,2:T(8,128)S(1)} %copy.249, s32[1024]{0:T(1024)S(1)} %get-tuple-element.363), kind=kCustom, calls=%fused_computation.4 | custom fusion | bytes 528384 | tf_op jit(solution)/shard_map/vmap()/gather | solution.py:111
  260.5 2.8 copy.250
  265.1 40.3 %psum.74 = f32[]{:T(128)} all-reduce(f32[]{:T(128)} %fusion.205), channel_id=1, replica_groups=mesh['chan'=8,'stn'=4] {'chan','stn'}, use_global_device_ids=true, to_apply=%region_37.0 | all-reduce | flops 1 | bytes 8 | tf_op jit(solution)/shard_map/psum | solution.py:241
  312.1 7.3 %all-reduce.14.cloned.1.call-done = f32[3,8,8,512]{3,2,1,0:T(8,128)} async-done(((f32[3,8,8,512]{3,2,1,0:T(8,128)}), f32[3,8,8,512]{3,2,1,0:T(8,128)}) %all-reduce.14.cloned.1.call-update) | async-done | bytes 393232 | tf_op jit(solution)/shard_map/psum | solution.py:251
  321.5 34.4 %all-reduce.12.cloned.1.call-done = f32[1,12,8,512]{3,2,0,1:T(8,128)} async-done(((f32[1,12,8,512]{3,2,0,1:T(8,128)}), f32[1,12,8,512]{3,2,0,1:T(8,128)}) %all-reduce.12.cloned.1.call-update) | async-done | bytes 196624 | tf_op jit(solution)/shard_map/psum | solution.py:245
  360.0 9.1 %gather_fusion.7 = f32[1024,8,8]{2,1,0:T(8,128)} fusion(f32[8,8,512]{1,0,2:T(8,128)S(1)} %copy.264, s32[1024]{0:T(1024)S(1)} %get-tuple-element.362), kind=kCustom, calls=%fused_computation.7 | custom fusion | bytes 528384 | tf_op jit(solution)/shard_map/vmap()/gather | solution.py:112
  369.2 9.1 %gather_fusion.6 = f32[1024,8,8]{2,1,0:T(8,128)} fusion(f32[8,8,512]{1,0,2:T(8,128)S(1)} %copy.264, s32[1024]{0:T(1024)S(1)} %get-tuple-element.363), kind=kCustom, calls=%fused_computation.6 | custom fusion | bytes 528384 | tf_op jit(solution)/shard_map/vmap()/gather | solution.py:111
  381.1 2.8 copy.265
  384.9 40.3 %psum.77 = f32[]{:T(128)} all-reduce(f32[]{:T(128)} %fusion.204), channel_id=1, replica_groups=mesh['chan'=8,'stn'=4] {'chan','stn'}, use_global_device_ids=true, to_apply=%region_49.0 | all-reduce | flops 1 | bytes 8 | tf_op jit(solution)/shard_map/psum | solution.py:241
  431.6 34.9 %all-reduce.16.cloned.1.call-done = f32[1,12,8,512]{3,2,0,1:T(8,128)} async-done(((f32[1,12,8,512]{3,2,0,1:T(8,128)}), f32[1,12,8,512]{3,2,0,1:T(8,128)}) %all-reduce.16.cloned.1.call-update) | async-done | bytes 196624 | tf_op jit(solution)/shard_map/psum | solution.py:245
  470.9 53.6 %all-reduce.18.cloned.1.call-done = f32[3,8,8,512]{3,2,1,0:T(8,128)} async-done(((f32[3,8,8,512]{3,2,1,0:T(8,128)}), f32[3,8,8,512]{3,2,1,0:T(8,128)}) %all-reduce.18.cloned.1.call-update) | async-done | bytes 393232 | tf_op jit(solution)/shard_map/psum | solution.py:251
  (253 shorter events, 68.5 us)
Async XLA Ops:
  7.2 29.5 %copy-start = (f32[1,8,16,1024]{3,2,1,0:T(8,128)S(1)}, f32[1,8,16,1024]{3,2,1,0:T(8,128)}, u32[]{:S(2)}) copy-start(f32[1,8,16,1024]{3,2,1,0:T(8,128)} %param.17) | copy-start | bytes 1572868
  7.2 116.8 %all-reduce.8.cloned.1.call-start = ((), (), s32[]{:S(2)}) async-start(), calls=%async_computation | async-start | bytes 393216 | tf_op jit(solution)/shard_map/psum | solution.py:245
  21.9 14.7 %copy-start.17 = (s32[16,1]{0,1:T(1,128)S(1)}, s32[16,1]{0,1:T(1,128)}, u32[]{:S(2)}) copy-start(s32[16,1]{0,1:T(1,128)} %param.18) | copy-start | bytes 196
  33.8 3.5 copy-start.1
  37.1 44.4 %copy-start.16 = (s32[4]{0:T(128)S(1)}, s32[4]{0:T(128)}, u32[]{:S(2)}) copy-start(s32[4]{0:T(128)} %constant.139.clone.1) | copy-start | bytes 52
  37.3 58.2 %copy-start.7 = (f32[3,8,8,512]{3,2,1,0:T(8,128)S(1)}, f32[3,8,8,512]{3,2,1,0:T(8,128)}, u32[]{:S(2)}) copy-start(f32[3,8,8,512]{3,2,1,0:T(8,128)} %param.21) | copy-start | bytes 1179652
  80.8 43.2 %copy-start.5 = (f32[1,8,8,512]{3,2,1,0:T(8,128)S(1)}, f32[1,8,8,512]{3,2,1,0:T(8,128)}, u32[]{:S(2)}) copy-start(f32[1,8,8,512]{3,2,1,0:T(8,128)} %param.22) | copy-start | bytes 393220
  80.8 43.2 %copy-start.14 = (f32[8]{0:T(128)S(1)}, f32[8]{0:T(128)}, u32[]{:S(2)}) copy-start(f32[8]{0:T(128)} %param.23) | copy-start | bytes 100
  81.1 45.7 %copy-start.6 = (f32[1,8,8,512]{3,2,1,0:T(8,128)S(1)}, f32[1,8,8,512]{3,2,1,0:T(8,128)}, u32[]{:S(2)}) copy-start(f32[1,8,8,512]{3,2,1,0:T(8,128)} %param.20) | copy-start | bytes 393220
  81.5 1.4 copy-start.15
  88.2 0.7 copy-start.12
  88.9 146.9 %all-reduce.10.cloned.1.call-start = ((), (), s32[]{:S(2)}) async-start(), calls=%async_computation.1 | async-start | bytes 393216 | tf_op jit(solution)/shard_map/psum | solution.py:245
  200.1 0.7 copy-start.13
  200.8 118.5 %all-reduce.14.cloned.1.call-start = ((), (), s32[]{:S(2)}) async-start(), calls=%async_computation.3 | async-start | bytes 786432 | tf_op jit(solution)/shard_map/psum | solution.py:251
  238.6 9.9 %copy-start.2 = (f32[1,8,8,512]{3,2,1,0:T(8,128)}, f32[1,8,8,512]{3,2,1,0:T(8,128)S(1)}, u32[]{:S(2)}) copy-start(f32[1,8,8,512]{3,2,1,0:T(8,128)S(1)} %get-tuple-element.150) | copy-start | bytes 393220
  265.0 90.8 %all-reduce.12.cloned.1.call-start = ((), (), s32[]{:S(2)}) async-start(), calls=%async_computation.2 | async-start | bytes 393216 | tf_op jit(solution)/shard_map/psum | solution.py:245
  306.4 52.8 %copy-start.3 = (f32[1,8,8,512]{3,2,1,0:T(8,128)S(1)}, f32[1,8,8,512]{3,2,1,0:T(8,128)}, u32[]{:S(2)}) copy-start(f32[1,8,8,512]{3,2,1,0:T(8,128)} %copy-done.2) | copy-start | bytes 393220
  311.1 0.7 copy-start.10
  311.8 154.7 %all-reduce.16.cloned.1.call-start = ((), (), s32[]{:S(2)}) async-start(), calls=%async_computation.4 | async-start | bytes 393216 | tf_op jit(solution)/shard_map/psum | solution.py:245
  358.6 0.6 copy-start.8
  426.0 43.3 %copy-start.4 = (f32[1,8,8,512]{3,2,1,0:T(8,128)S(1)}, f32[1,8,8,512]{3,2,1,0:T(8,128)}, u32[]{:S(2)}) copy-start(f32[1,8,8,512]{3,2,1,0:T(8,128)} %copy-done.2) | copy-start | bytes 393220
  426.0 43.3 %copy-start.9 = (f32[8,1,8,512]{3,2,0,1:T(8,128)S(1)}, f32[8,1,8,512]{3,2,0,1:T(8,128)}, u32[]{:S(2)}) copy-start(f32[8,1,8,512]{3,2,0,1:T(8,128)} %copy-done.8) | copy-start | bytes 393220
  430.9 0.7 copy-start.11
  431.6 92.9 %all-reduce.18.cloned.1.call-start = ((), (), s32[]{:S(2)}) async-start(), calls=%async_computation.5 | async-start | bytes 786432 | tf_op jit(solution)/shard_map/psum | solution.py:251
Sparse Core Ops, SparseCore 0:
  89.0 34.9 all-reduce.7
  200.9 34.8 all-reduce.9
  265.2 54.1 all-reduce.13
  321.5 34.3 all-reduce.11
  431.7 34.8 all-reduce.15
  470.4 54.0 all-reduce.17
where the time goes:
time: 538 us; the launch traced here: 535 us
  waiting for transfers between devices  192 us (36%)
  blocking collectives  163 us (30%)
  local copies, waits for them, and re-layouts  111 us (21%)
  other arithmetic  28.8 us (5%)
  between operations  21.2 us (4%)
  matrix products  17.9 us (3%)
    psum x4, blocking collectives, body(): lax.psum(jnp.sum(chan_state[5]), ('chan', 'stn')) / sample_count  163 us
    psum x4, waiting for transfers between devices, body(): whole_accumulated_totals = lax.psum(least_squares_equations, 'stn')  132 us
    psum x2, waiting for transfers between devices, body(): fit_now = lax.psum(partial_fit, 'chan') / total_ch  60.8 us
    gather x8, local copies, waits for them, and re-layouts, channel_state(): second_gain = entries(spectral_jones_matrices[:, :, antenna_pairs[1]])  47.6 us
    gather x8, local copies, waits for them, and re-layouts, channel_state(): first_gain = entries(spectral_jones_matrices[:, :, antenna_pairs[0]])  47.5 us
  transfers between devices with their start and end apart: 6, of which 6 were waited for; matrix products, arithmetic and copies ran while one was open for 2% of the time, Pallas kernels for 0%

commit v1 on v0

--- a/solution.py
+++ b/solution.py
@@ -11,6 +11,12 @@
 student_nu = 2.0
 squared_tolerance = 1e-06
 highest = lax.Precision.HIGHEST
+
+
+def gather_and_add(x, name):
+    parts = lax.all_gather(x, name, axis=0, tiled=False)
+    result = parts.sum(axis=0)
+    return result
 
 
 def entries(stacked):
@@ -242,7 +248,7 @@
             )
             weight = (student_nu + 2.0) / (student_nu + chan_state[5] / mean_square)
             least_squares_equations = sums_fn(chan_state, weight)
-            whole_accumulated_totals = lax.psum(least_squares_equations, "stn")
+            whole_accumulated_totals = gather_and_add(least_squares_equations, "stn")
             whole_jones_matrix = estimate_routine(
                 whole_accumulated_totals, pivot_antenna, whole_jones_matrix, augmented_lagrange_rhos
             )

time: 538 us -> 455 us (0.85)
  waiting for transfers between devices: 192 us -> 55.1 us
  blocking collectives: 163 us -> 233 us
  other arithmetic: 28.8 us -> 20 us
    psum x4 -> x0, waiting for transfers between devices: 132 us -> none  [body(): whole_accumulated_totals = lax.psum(least_squares_equations, 'stn')]
    all_gather x0 -> x4, blocking collectives: none -> 72.8 us  [gather_and_add(): parts = lax.all_gather(x, name, axis=0, tiled=False)]
    psum x2, waiting for transfers between devices: 60.8 us -> 55.1 us  [body(): fit_now = lax.psum(partial_fit, 'chan') / total_ch]
    unnamed x113, other arithmetic: 9.72 us -> 4.31 us
  transfers between devices with their start and end apart: 6 -> 2, of which waited for: 6 -> 1; matrix products, arithmetic and copies ran while one was open for 2% -> 7% of each run, Pallas kernels for 0% -> 0%
where the time goes in v1:
time: 455 us; the launch traced here: 454 us
  blocking collectives  233 us (51%)
  local copies, waits for them, and re-layouts  108 us (24%)
  waiting for transfers between devices  55.1 us (12%)
  between operations  21.1 us (5%)
  other arithmetic  20 us (4%)
  matrix products  17 us (4%)
    psum x4, blocking collectives, body(): lax.psum(jnp.sum(chan_state[5]), ('chan', 'stn')) / sample_count  160 us
    all_gather x4, blocking collectives, gather_and_add(): parts = lax.all_gather(x, name, axis=0, tiled=False)  72.8 us
    psum x2, waiting for transfers between devices, body(): fit_now = lax.psum(partial_fit, 'chan') / total_ch  55.1 us
    gather x8, local copies, waits for them, and re-layouts, channel_state(): second_gain = entries(spectral_jones_matrices[:, :, antenna_pairs[1]])  47.6 us
    gather x8, local copies, waits for them, and re-layouts, channel_state(): first_gain = entries(spectral_jones_matrices[:, :, antenna_pairs[0]])  47.5 us
    dot_general x4, matrix products, channel_sums(): jnp.einsum('pkb,bs->pks', first_parts, first_table, precision=highest)  9.5 us
  transfers between devices with their start and end apart: 2, of which 1 were waited for; matrix products, arithmetic and copies ran while one was open for 7% of the time, Pallas kernels for 0%

profile of v1, /device:TPU:0, one launch (start us, length us, event | category | flops | bytes accessed | tf_op | source)
XLA Modules:
  0.0 454.1 jit_solution(10579202551962642939)
XLA Ops:
  19.3 9.1 %gather_fusion.1 = f32[1024,8,8]{2,1,0:T(8,128)} fusion(f32[8,8,512]{1,0,2:T(8,128)S(1)} %bitcast.889, s32[1024]{0:T(1024)S(1)} %get-tuple-element.371), kind=kCustom, calls=%fused_computation.1 | custom fusion | bytes 528384 | tf_op jit(solution)/shard_map/vmap()/gather | solution.py:118
  28.4 2.8 copy.780
  31.2 9.1 %gather_fusion = f32[1024,8,8]{2,1,0:T(8,128)} fusion(f32[8,8,512]{1,0,2:T(8,128)S(1)} %bitcast.890, s32[1024]{0:T(1024)S(1)} %get-tuple-element.372), kind=kCustom, calls=%fused_computation | custom fusion | bytes 528384 | tf_op jit(solution)/shard_map/vmap()/gather | solution.py:117
  40.3 2.8 copy.768
  45.6 42.2 %psum.42 = f32[]{:T(128)} all-reduce(f32[]{:T(128)} %fusion.199), channel_id=1, replica_groups=mesh['chan'=8,'stn'=4] {'chan','stn'}, use_global_device_ids=true, to_apply=%region_9.0 | all-reduce | flops 1 | bytes 8 | tf_op jit(solution)/shard_map/psum | solution.py:247
  94.3 18.1 %all_gather.34 = f32[4,1,12,8,512]{4,3,2,1,0:T(8,128)S(1)} all-gather(f32[1,1,12,8,512]{4,3,2,1,0:T(8,128)S(1)} %scatter.14), channel_id=1, replica_groups=mesh['chan'=8,'stn'=4] {'stn'}, dimensions={0}, use_global_device_ids=true | all-gather | bytes 983040 | tf_op jit(solution)/shard_map/all_gather | solution.py:17
  116.4 9.1 %gather_fusion.3 = f32[1024,8,8]{2,1,0:T(8,128)} fusion(f32[8,8,512]{1,0,2:T(8,128)S(1)} %copy.785, s32[1024]{0:T(1024)S(1)} %get-tuple-element.371), kind=kCustom, calls=%fused_computation.3 | custom fusion | bytes 528384 | tf_op jit(solution)/shard_map/vmap()/gather | solution.py:118
  125.5 9.1 %gather_fusion.2 = f32[1024,8,8]{2,1,0:T(8,128)} fusion(f32[8,8,512]{1,0,2:T(8,128)S(1)} %copy.785, s32[1024]{0:T(1024)S(1)} %get-tuple-element.372), kind=kCustom, calls=%fused_computation.2 | custom fusion | bytes 528384 | tf_op jit(solution)/shard_map/vmap()/gather | solution.py:117
  134.6 2.8 copy.792
  137.5 2.8 copy.786
  141.2 38.9 %psum.43 = f32[]{:T(128)} all-reduce(f32[]{:T(128)} %fusion.198), channel_id=1, replica_groups=mesh['chan'=8,'stn'=4] {'chan','stn'}, use_global_device_ids=true, to_apply=%region_26.0 | all-reduce | flops 1 | bytes 8 | tf_op jit(solution)/shard_map/psum | solution.py:247
  185.9 18.2 %all_gather.37 = f32[4,1,12,8,512]{4,3,2,1,0:T(8,128)S(1)} all-gather(f32[1,1,12,8,512]{4,3,2,1,0:T(8,128)S(1)} %scatter.15), channel_id=1, replica_groups=mesh['chan'=8,'stn'=4] {'stn'}, dimensions={0}, use_global_device_ids=true | all-gather | bytes 983040 | tf_op jit(solution)/shard_map/all_gather | solution.py:17
  206.3 9.1 %gather_fusion.5 = f32[1024,8,8]{2,1,0:T(8,128)} fusion(f32[8,8,512]{1,0,2:T(8,128)S(1)} %copy.797, s32[1024]{0:T(1024)S(1)} %get-tuple-element.371), kind=kCustom, calls=%fused_computation.5 | custom fusion | bytes 528384 | tf_op jit(solution)/shard_map/vmap()/gather | solution.py:118
  215.4 9.1 %gather_fusion.4 = f32[1024,8,8]{2,1,0:T(8,128)} fusion(f32[8,8,512]{1,0,2:T(8,128)S(1)} %copy.797, s32[1024]{0:T(1024)S(1)} %get-tuple-element.372), kind=kCustom, calls=%fused_computation.4 | custom fusion | bytes 528384 | tf_op jit(solution)/shard_map/vmap()/gather | solution.py:117
  227.4 2.8 copy.798
  231.1 40.0 %psum.44 = f32[]{:T(128)} all-reduce(f32[]{:T(128)} %fusion.197), channel_id=1, replica_groups=mesh['chan'=8,'stn'=4] {'chan','stn'}, use_global_device_ids=true, to_apply=%region_37.0 | all-reduce | flops 1 | bytes 8 | tf_op jit(solution)/shard_map/psum | solution.py:247
  276.8 18.4 %all_gather.40 = f32[4,1,12,8,512]{4,3,2,1,0:T(8,128)S(1)} all-gather(f32[1,1,12,8,512]{4,3,2,1,0:T(8,128)S(1)} %scatter.16), channel_id=1, replica_groups=mesh['chan'=8,'stn'=4] {'stn'}, dimensions={0}, use_global_device_ids=true | all-gather | bytes 983040 | tf_op jit(solution)/shard_map/all_gather | solution.py:17
  299.3 9.1 %gather_fusion.7 = f32[1024,8,8]{2,1,0:T(8,128)} fusion(f32[8,8,512]{1,0,2:T(8,128)S(1)} %copy.809, s32[1024]{0:T(1024)S(1)} %get-tuple-element.371), kind=kCustom, calls=%fused_computation.7 | custom fusion | bytes 528384 | tf_op jit(solution)/shard_map/vmap()/gather | solution.py:118
  308.4 9.1 %gather_fusion.6 = f32[1024,8,8]{2,1,0:T(8,128)} fusion(f32[8,8,512]{1,0,2:T(8,128)S(1)} %copy.809, s32[1024]{0:T(1024)S(1)} %get-tuple-element.372), kind=kCustom, calls=%fused_computation.6 | custom fusion | bytes 528384 | tf_op jit(solution)/shard_map/vmap()/gather | solution.py:117
  317.5 2.8 copy.816
  320.4 2.8 copy.810
  324.1 38.8 %psum.46 = f32[]{:T(128)} all-reduce(f32[]{:T(128)} %fusion.196), channel_id=1, replica_groups=mesh['chan'=8,'stn'=4] {'chan','stn'}, use_global_device_ids=true, to_apply=%region_49.0 | all-reduce | flops 1 | bytes 8 | tf_op jit(solution)/shard_map/psum | solution.py:247
  368.6 18.1 %all_gather.43 = f32[4,1,12,8,512]{4,3,2,1,0:T(8,128)S(1)} all-gather(f32[1,1,12,8,512]{4,3,2,1,0:T(8,128)S(1)} %scatter.19), channel_id=1, replica_groups=mesh['chan'=8,'stn'=4] {'stn'}, dimensions={0}, use_global_device_ids=true | all-gather | bytes 983040 | tf_op jit(solution)/shard_map/all_gather | solution.py:17
  388.7 55.0 %all-reduce.6.cloned.1.call-done = f32[3,8,8,512]{3,2,1,0:T(8,128)} async-done(((f32[3,8,8,512]{3,2,1,0:T(8,128)}), f32[3,8,8,512]{3,2,1,0:T(8,128)}) %all-reduce.6.cloned.1.call-update) | async-done | bytes 393232 | tf_op jit(solution)/shard_map/psum | solution.py:257
  (241 shorter events, 53.0 us)
Async XLA Ops:
  7.2 35.9 %copy-start = (f32[1,8,16,1024]{3,2,1,0:T(8,128)S(1)}, f32[1,8,16,1024]{3,2,1,0:T(8,128)}, u32[]{:S(2)}) copy-start(f32[1,8,16,1024]{3,2,1,0:T(8,128)} %param.17) | copy-start | bytes 1572868
  7.2 288.1 %all-reduce.4.cloned.1.call-start = ((), (), s32[]{:S(2)}) async-start(), calls=%async_computation | async-start | bytes 786432 | tf_op jit(solution)/shard_map/psum | solution.py:257
  28.4 14.7 %copy-start.13 = (s32[16,1]{0,1:T(1,128)S(1)}, s32[16,1]{0,1:T(1,128)}, u32[]{:S(2)}) copy-start(s32[16,1]{0,1:T(1,128)} %param.18) | copy-start | bytes 196
  40.3 4.1 copy-start.1
  44.1 44.0 %copy-start.11 = (f32[12,1,8,1024]{3,2,0,1:T(8,128)S(1)}, f32[12,1,8,1024]{3,2,0,1:T(8,128)}, u32[]{:S(2)}) copy-start(f32[12,1,8,1024]{3,2,0,1:T(8,128)} %get-tuple-element.279) | copy-start | bytes 1179652
  44.1 44.4 %copy-start.12 = (s32[4]{0:T(128)S(1)}, s32[4]{0:T(128)}, u32[]{:S(2)}) copy-start(s32[4]{0:T(128)} %constant.143.clone.1) | copy-start | bytes 52
  88.0 24.6 %copy-start.7 = (f32[3,8,8,512]{3,2,1,0:T(8,128)S(1)}, f32[3,8,8,512]{3,2,1,0:T(8,128)}, u32[]{:S(2)}) copy-start(f32[3,8,8,512]{3,2,1,0:T(8,128)} %param.21) | copy-start | bytes 1179652
  88.1 25.7 %copy-start.5 = (f32[1,8,8,512]{3,2,1,0:T(8,128)S(1)}, f32[1,8,8,512]{3,2,1,0:T(8,128)}, u32[]{:S(2)}) copy-start(f32[1,8,8,512]{3,2,1,0:T(8,128)} %param.22) | copy-start | bytes 393220
  88.1 25.7 %copy-start.10 = (f32[8]{0:T(128)S(1)}, f32[8]{0:T(128)}, u32[]{:S(2)}) copy-start(f32[8]{0:T(128)} %param.23) | copy-start | bytes 100
  88.3 25.8 %copy-start.6 = (f32[1,8,8,512]{3,2,1,0:T(8,128)S(1)}, f32[1,8,8,512]{3,2,1,0:T(8,128)}, u32[]{:S(2)}) copy-start(f32[1,8,8,512]{3,2,1,0:T(8,128)} %param.20) | copy-start | bytes 393220
  204.5 10.8 %copy-start.2 = (f32[1,8,8,512]{3,2,1,0:T(8,128)}, f32[1,8,8,512]{3,2,1,0:T(8,128)S(1)}, u32[]{:S(2)}) copy-start(f32[1,8,8,512]{3,2,1,0:T(8,128)S(1)} %get-tuple-element.159) | copy-start | bytes 393220
  205.5 238.3 %all-reduce.6.cloned.1.call-start = ((), (), s32[]{:S(2)}) async-start(), calls=%async_computation.1 | async-start | bytes 786432 | tf_op jit(solution)/shard_map/psum | solution.py:257
  272.3 26.2 %copy-start.3 = (f32[1,8,8,512]{3,2,1,0:T(8,128)S(1)}, f32[1,8,8,512]{3,2,1,0:T(8,128)}, u32[]{:S(2)}) copy-start(f32[1,8,8,512]{3,2,1,0:T(8,128)} %copy-done.2) | copy-start | bytes 393220
  297.8 0.7 copy-start.8
  363.9 23.2 %copy-start.4 = (f32[1,8,8,512]{3,2,1,0:T(8,128)S(1)}, f32[1,8,8,512]{3,2,1,0:T(8,128)}, u32[]{:S(2)}) copy-start(f32[1,8,8,512]{3,2,1,0:T(8,128)} %copy-done.2) | copy-start | bytes 393220
  363.9 23.2 %copy-start.9 = (f32[8,1,8,512]{3,2,1,0:T(8,128)S(1)}, f32[8,1,8,512]{3,2,1,0:T(8,128)}, u32[]{:S(2)}) copy-start(f32[8,1,8,512]{3,2,1,0:T(8,128)} %copy-done.8) | copy-start | bytes 393220
Sparse Core Ops, SparseCore 0:
  205.6 55.1 all-reduce.3
  388.2 55.5 all-reduce.5
